TPU v7x, 256 devices: a whole 4x4x8 slice. The times are simulated.
256 devices in a mesh: row: 8 (over x, y_lo), col: 32 (over y_hi, z, core).
Axes of the slice: x: 4, y: 4 (y_hi: 2, y_lo: 2; y = y_hi * 2 + y_lo), z: 8, core: 2. Of those that a mesh axis runs over, the one named last changes fastest.
Arguments:
- features: bfloat16 [32768, 512], P(('col', 'row')), may hold values from -6 to 6
- tile_vals: bfloat16 [8, 4096, 128, 128], P('row', 'col')
- tile_row: int32 [8, 4096], P('row', 'col'), may hold values from 0 to 31
- tile_col: int32 [8, 4096], P('row', 'col'), may hold values from 0 to 7
- tile_count: int32 [8, 32], P('row', 'col'), may hold values from 1 to 128, as said below
- node_type: int32 [32768], P(('row', 'col')), may hold values from 0 to 7
- type_gain: float32 [8, 512], replicated, may hold values from 0.1 to 1.9
- w_in: bfloat16 [512, 1024], replicated, may hold values from -0.25 to 0.25
- w_out: bfloat16 [1024, 512], replicated, may hold values from -0.1875 to 0.1875
- cotangent: bfloat16 [32768, 512], P(('row', 'col')), may hold values from -6 to 6
Outputs:
- mixed: bfloat16 [32768, 512], P(('row', 'col'))
- grad_x: float32 [32768, 512], P(('col', 'row'))
- grad_w_in: float32 [512, 1024], replicated
- grad_w_out: float32 [1024, 512], replicated
- grad_gain: float32 [8, 512], replicated
Inputs may be any that keep to these rules, and one draw needn't show every extreme that they name: Slots 0 to tile_count - 1 of a grid cell's list are live; some grid cell has all 128 slots live in every draw.
All inputs are finite; a program needn't handle non-finite values.
Results may differ from a plain program's by a relative error of at most 0.0056.
Values may be sent and summed in bfloat16 or wider, within the bound.
A program may use at most 128 MiB of HBM per device.

v0:
```python
import jax
import jax.numpy as jnp
from jax import lax
from jax.sharding import PartitionSpec as P

F = 512
TYPES = 8
TILE = 128


def sweep(weights_all, row_ids_all, col_ids_all, live_count, sources, target, forward, lower):
    span = target.shape[0]
    rounds = weights_all.shape[0] // 16

    def advance(block_index, totals):
        first_slot = block_index * 16
        weights_now = lax.dynamic_slice_in_dim(weights_all, first_slot, 16, 0)
        row_ids = lax.dynamic_slice_in_dim(row_ids_all, first_slot, 16, 0)
        col_ids = lax.dynamic_slice_in_dim(col_ids_all, first_slot, 16, 0)
        living = first_slot + jnp.arange(16, dtype=jnp.int32) < live_count
        if forward:
            pieces = sources[col_ids]
            product = jnp.einsum(
                "sab,sbf->saf", weights_now, pieces, preferred_element_type=jnp.float32
            )
            destination = row_ids - lower
        else:
            pieces = sources[row_ids]
            product = jnp.einsum(
                "sab,saf->sbf", weights_now, pieces, preferred_element_type=jnp.float32
            )
            destination = col_ids - lower
        inside = living & (destination >= 0) & (destination < span)
        product = jnp.where(inside[:, None, None], product, 0.0)
        placed = jnp.clip(destination, 0, span - 1)
        return totals.at[placed].add(product)

    return lax.fori_loop(0, rounds, advance, target)


def shards(
    features,
    tile_vals,
    tile_row,
    tile_col,
    tile_count,
    node_type,
    type_gain,
    w_in,
    w_out,
    cotangent,
):
    row_count = lax.axis_size("row")
    col_count = lax.axis_size("col")
    total_nodes = TILE * row_count * col_count
    weights_all = tile_vals[0]
    row_ids_all = tile_row[0]
    col_ids_all = tile_col[0]
    live_count = tile_count[0, 0]
    gathered = lax.all_gather(features, "row", axis=0, tiled=True).reshape(row_count, TILE, F)
    totals = sweep(
        weights_all,
        row_ids_all,
        col_ids_all,
        live_count,
        gathered,
        jnp.zeros((col_count, TILE, F), jnp.float32),
        True,
        0,
    )
    aggregate = lax.psum_scatter(
        totals.reshape(col_count * TILE, F), "col", scatter_dimension=0, tiled=True
    )
    center = jnp.mean(aggregate, axis=-1, keepdims=True)
    spread = jnp.mean(jnp.square(aggregate - center), axis=-1, keepdims=True)
    inverse = lax.rsqrt(spread + 1e-05)
    normed = (aggregate - center) * inverse
    onehot = (node_type[:, None] == jnp.arange(TYPES, dtype=jnp.int32)[None, :]).astype(jnp.float32)
    gains = jnp.dot(onehot, type_gain, precision=lax.Precision.HIGHEST)
    scaled = (normed * gains).astype(jnp.bfloat16)
    hidden = jnp.dot(scaled, w_in, preferred_element_type=jnp.float32)
    activated = jax.nn.silu(hidden).astype(jnp.bfloat16)
    branch = jnp.dot(activated, w_out, preferred_element_type=jnp.float32)
    mixed = (aggregate + branch).astype(jnp.bfloat16)
    upstream = cotangent.astype(jnp.float32)
    grad_out_w = jnp.dot(activated.T, cotangent, preferred_element_type=jnp.float32)
    grad_act = jnp.dot(cotangent, w_out.T, preferred_element_type=jnp.float32)
    sigmoid_h = jax.nn.sigmoid(hidden)
    grad_hidden = (grad_act * sigmoid_h * (1.0 + hidden * (1.0 - sigmoid_h))).astype(jnp.bfloat16)
    grad_in_w = jnp.dot(scaled.T, grad_hidden, preferred_element_type=jnp.float32)
    grad_scaled = jnp.dot(grad_hidden, w_in.T, preferred_element_type=jnp.float32)
    grad_gain = jnp.dot(onehot.T, grad_scaled * normed, precision=lax.Precision.HIGHEST)
    grad_normed = grad_scaled * gains
    grad_agg = upstream + inverse * (
        grad_normed
        - jnp.mean(grad_normed, axis=-1, keepdims=True)
        - normed * jnp.mean(grad_normed * normed, axis=-1, keepdims=True)
    )
    grad_rows = grad_agg.astype(jnp.bfloat16)
    reduced = lax.psum((grad_in_w, grad_out_w, grad_gain), ("row", "col"))
    grad_sources = lax.all_gather(grad_rows, "col", axis=0, tiled=True).reshape(col_count, TILE, F)
    back = sweep(
        weights_all,
        row_ids_all,
        col_ids_all,
        live_count,
        grad_sources,
        jnp.zeros((row_count, TILE, F), jnp.float32),
        False,
        0,
    )
    grad_x = lax.psum_scatter(
        back.reshape(row_count * TILE, F), "row", scatter_dimension=0, tiled=True
    )
    factor = float(total_nodes) ** (-0.5)
    return (mixed, grad_x, reduced[0] * factor, reduced[1] * factor, reduced[2] * factor)


def solution(mesh):
    return jax.shard_map(
        shards,
        mesh=mesh,
        in_specs=(
            P(("col", "row"), None),
            P("row", "col", None, None),
            P("row", "col"),
            P("row", "col"),
            P("row", "col"),
            P(("row", "col")),
            P(),
            P(),
            P(),
            P(("row", "col"), None),
        ),
        out_specs=(P(("row", "col"), None), P(("col", "row"), None), P(), P(), P()),
        check_vma=False,
    )
```

profile of v0, /device:TPU:32, one launch (start us, length us, event | category | flops | bytes accessed | tf_op | source)
XLA Modules:
  0.0 769.9 jit_solution(11946579066212321571)
XLA Ops:
  8.0 45.8 %all-gather.3.cloned.1.call-done = bf16[1024,512]{1,0:T(8,128)(2,1)} async-done(((bf16[128,512]{1,0:T(8,128)(2,1)}), bf16[1024,512]{1,0:T(8,128)(2,1)}) %all-gather.3.cloned.1.call-update) | async-done | bytes 1048592 | tf_op jit(solution)/shard_map/all_gather | solution.py:60
  53.8 4.3 broadcast_in_dim.90
  58.1 127.6 %while.26 = (s32[]{:T(128)}, f32[32,128,512]{2,1,0:T(8,128)}, s32[128]{0:T(128)S(1)}, s32[]{:T(128)}, bf16[128,128,128]{2,1,0:T(8,128)(2,1)}, /*index=5*/s32[128...) while((s32[]{:T(128)}, f32[32,128,512]{2,1,0:T(8,128)}, ...), condition=%wide.region_2.3_spmd, body=%wide.region_0.2_spmd.sunk | while | flops 270533856 | bytes 23597776 | solution.py:38
  60.8 3.7 convolution_select_fusion.4
  64.5 9.6 %scatter_fusion = f32[32,128,512]{2,1,0:T(8,128)} fusion(f32[32,128,512]{2,1,0:T(8,128)} %get-tuple-element.410, s32[16]{0:T(128)S(1)} %get-tuple-element.387, f32[16,128,512]{2,1,0:T(8,128)} %convolution_select_fusion.4), kind=kCustom, calls=%fused_computation.2.clone.1 | custom fusion | flops 1048576 | bytes 12582976 | tf_op jit(solution)/shard_map/while/body/eval_jaxpr/scatter-add | solution.py:36
  76.8 3.7 convolution_select_fusion.4
  80.5 9.6 %scatter_fusion = f32[32,128,512]{2,1,0:T(8,128)} fusion(f32[32,128,512]{2,1,0:T(8,128)} %get-tuple-element.410, s32[16]{0:T(128)S(1)} %get-tuple-element.387, f32[16,128,512]{2,1,0:T(8,128)} %convolution_select_fusion.4), kind=kCustom, calls=%fused_computation.2.clone.1 | custom fusion | flops 1048576 | bytes 12582976 | tf_op jit(solution)/shard_map/while/body/eval_jaxpr/scatter-add | solution.py:36
  92.8 3.7 convolution_select_fusion.4
  96.5 9.5 %scatter_fusion = f32[32,128,512]{2,1,0:T(8,128)} fusion(f32[32,128,512]{2,1,0:T(8,128)} %get-tuple-element.410, s32[16]{0:T(128)S(1)} %get-tuple-element.387, f32[16,128,512]{2,1,0:T(8,128)} %convolution_select_fusion.4), kind=kCustom, calls=%fused_computation.2.clone.1 | custom fusion | flops 1048576 | bytes 12582976 | tf_op jit(solution)/shard_map/while/body/eval_jaxpr/scatter-add | solution.py:36
  108.6 3.7 convolution_select_fusion.4
  112.3 9.5 %scatter_fusion = f32[32,128,512]{2,1,0:T(8,128)} fusion(f32[32,128,512]{2,1,0:T(8,128)} %get-tuple-element.410, s32[16]{0:T(128)S(1)} %get-tuple-element.387, f32[16,128,512]{2,1,0:T(8,128)} %convolution_select_fusion.4), kind=kCustom, calls=%fused_computation.2.clone.1 | custom fusion | flops 1048576 | bytes 12582976 | tf_op jit(solution)/shard_map/while/body/eval_jaxpr/scatter-add | solution.py:36
  128.2 9.7 %scatter_fusion = f32[32,128,512]{2,1,0:T(8,128)} fusion(f32[32,128,512]{2,1,0:T(8,128)} %get-tuple-element.410, s32[16]{0:T(128)S(1)} %get-tuple-element.387, f32[16,128,512]{2,1,0:T(8,128)} %convolution_select_fusion.4), kind=kCustom, calls=%fused_computation.2.clone.1 | custom fusion | flops 1048576 | bytes 12582976 | tf_op jit(solution)/shard_map/while/body/eval_jaxpr/scatter-add | solution.py:36
  140.7 3.7 convolution_select_fusion.4
  144.4 9.5 %scatter_fusion = f32[32,128,512]{2,1,0:T(8,128)} fusion(f32[32,128,512]{2,1,0:T(8,128)} %get-tuple-element.410, s32[16]{0:T(128)S(1)} %get-tuple-element.387, f32[16,128,512]{2,1,0:T(8,128)} %convolution_select_fusion.4), kind=kCustom, calls=%fused_computation.2.clone.1 | custom fusion | flops 1048576 | bytes 12582976 | tf_op jit(solution)/shard_map/while/body/eval_jaxpr/scatter-add | solution.py:36
  160.3 9.4 %scatter_fusion = f32[32,128,512]{2,1,0:T(8,128)} fusion(f32[32,128,512]{2,1,0:T(8,128)} %get-tuple-element.410, s32[16]{0:T(128)S(1)} %get-tuple-element.387, f32[16,128,512]{2,1,0:T(8,128)} %convolution_select_fusion.4), kind=kCustom, calls=%fused_computation.2.clone.1 | custom fusion | flops 1048576 | bytes 12582976 | tf_op jit(solution)/shard_map/while/body/eval_jaxpr/scatter-add | solution.py:36
  172.4 3.7 convolution_select_fusion.4
  176.1 9.5 %scatter_fusion = f32[32,128,512]{2,1,0:T(8,128)} fusion(f32[32,128,512]{2,1,0:T(8,128)} %get-tuple-element.410, s32[16]{0:T(128)S(1)} %get-tuple-element.387, f32[16,128,512]{2,1,0:T(8,128)} %convolution_select_fusion.4), kind=kCustom, calls=%fused_computation.2.clone.1 | custom fusion | flops 1048576 | bytes 12582976 | tf_op jit(solution)/shard_map/while/body/eval_jaxpr/scatter-add | solution.py:36
  185.7 153.5 %reduce-scatter.3.cloned.1.call-done = f32[128,512]{1,0:T(8,128)} async-done(((f32[4096,512]{1,0:T(8,128)}), f32[128,512]{1,0:T(8,128)}) %reduce-scatter.3.cloned.1.call-update) | async-done | bytes 262160 | tf_op jit(solution)/shard_map/reduce_scatter | solution.py:71
  347.1 6.4 copy.15
  357.2 75.2 %all-gather.5.cloned.1.call-done = bf16[4096,512]{1,0:T(8,128)(2,1)} async-done(((bf16[128,512]{1,0:T(8,128)(2,1)}), bf16[4096,512]{1,0:T(8,128)(2,1)}) %all-gather.5.cloned.1.call-update) | async-done | bytes 4194320 | tf_op jit(solution)/shard_map/all_gather | solution.py:101
  432.7 125.2 %while.27 = (s32[]{:T(128)}, f32[8,128,512]{2,1,0:T(8,128)S(1)}, s32[128]{0:T(128)S(1)}, s32[]{:T(128)}, bf16[128,128,128]{1,2,0:T(8,128)(2,1)}, /*index=5*/s32[...) while((s32[]{:T(128)}, f32[8,128,512]{2,1,0:T(8,128)S(1)}, ...), condition=%wide.region_10.11_spmd, body=%wide.region_8.10_spmd.sunk | while | flops 270533856 | bytes 23597776 | solution.py:38
  433.5 4.2 gather_fusion.1
  437.7 4.4 convolution_select_fusion.5
  442.1 6.4 scatter_fusion.1
  449.4 4.2 gather_fusion.1
  453.6 4.4 convolution_select_fusion.5
  458.0 6.1 scatter_fusion.1
  465.0 4.2 gather_fusion.1
  469.2 4.4 convolution_select_fusion.5
  473.6 6.2 scatter_fusion.1
  480.7 4.2 gather_fusion.1
  484.9 4.4 convolution_select_fusion.5
  489.3 6.2 scatter_fusion.1
  496.3 4.2 gather_fusion.1
  500.5 4.4 convolution_select_fusion.5
  504.9 6.2 scatter_fusion.1
  511.9 4.2 gather_fusion.1
  516.1 4.4 convolution_select_fusion.5
  520.5 6.2 scatter_fusion.1
  527.6 4.2 gather_fusion.1
  531.8 4.4 convolution_select_fusion.5
  536.2 6.1 scatter_fusion.1
  543.2 4.2 gather_fusion.1
  547.4 4.4 convolution_select_fusion.5
  551.8 6.1 scatter_fusion.1
  560.6 75.6 %psum.23 = f32[8,512]{1,0:T(8,128)S(1)} all-reduce(f32[8,512]{1,0:T(8,128)S(1)} %fusion.7), channel_id=1, replica_groups=mesh['row'=8,'col'=32] {'row','col'}, use_global_device_ids=true, to_apply=%region_14.15 | all-reduce | flops 4096 | bytes 32768 | tf_op jit(solution)/shard_map/psum | solution.py:100
  639.2 65.0 %all-reduce.3.cloned.1.call-done = (f32[512,1024]{1,0:T(8,128)}, f32[1024,512]{1,0:T(8,128)}) async-done(((f32[512,1024]{1,0:T(8,128)}, f32[1024,512]{1,0:T(8,128)}), (f32[512,1024]{1,0:T(8,128)}, f32[1024,512]{1,0:T(8,128)})) %all-reduce.3.cloned.1.call-update) | async-done | bytes 4194320 | tf_op jit(solution)/shard_map/psum | solution.py:100
  709.0 54.3 %reduce-scatter.5.cloned.1.call-done = f32[128,512]{1,0:T(8,128)} async-done(((f32[1024,512]{1,0:T(8,128)}), f32[128,512]{1,0:T(8,128)}) %reduce-scatter.5.cloned.1.call-update) | async-done | bytes 262160 | tf_op jit(solution)/shard_map/reduce_scatter | solution.py:112
  (106 shorter events, 58.5 us)
Async XLA Ops:
  7.2 335.6 %copy-start = (bf16[512,1024]{1,0:T(8,128)(2,1)S(1)}, bf16[512,1024]{1,0:T(8,128)(2,1)}, u32[]{:S(2)}) copy-start(bf16[512,1024]{1,0:T(8,128)(2,1)} %param.21) | copy-start | bytes 3145732
  7.2 46.6 %all-gather.3.cloned.1.call-start = ((), (), s32[]{:S(2)}) async-start(), calls=%async_computation.2 | async-start | bytes 1179648 | tf_op jit(solution)/shard_map/all_gather | solution.py:60
  7.9 331.3 %reduce-scatter.3.cloned.1.call-start = ((), (), s32[]{:S(2)}) async-start(), calls=%async_computation.3 | async-start | bytes 8650752 | tf_op jit(solution)/shard_map/reduce_scatter | solution.py:71
  53.8 4.3 copy-start.6
  53.8 4.3 copy-start.7
  185.6 155.8 %copy-start.8 = (f32[8,512]{1,0:T(8,128)S(1)}, f32[8,512]{1,0:T(8,128)}, u32[]{:S(2)}) copy-start(f32[8,512]{1,0:T(8,128)} %param.20) | copy-start | bytes 49156
  185.6 155.8 %copy-start.9 = (s32[128]{0:T(128)S(1)}, s32[128]{0:T(128)}, u32[]{:S(2)}) copy-start(s32[128]{0:T(128)} %param.19) | copy-start | bytes 1540
  185.6 157.4 %copy-start.5 = (bf16[128,512]{1,0:T(8,128)(2,1)S(1)}, bf16[128,512]{1,0:T(8,128)(2,1)}, u32[]{:S(2)}) copy-start(bf16[128,512]{1,0:T(8,128)(2,1)} %param.23) | copy-start | bytes 393220
  185.6 246.8 %all-gather.5.cloned.1.call-start = ((), (), s32[]{:S(2)}) async-start(), calls=%async_computation.4 | async-start | bytes 4325376 | tf_op jit(solution)/shard_map/all_gather | solution.py:101
  343.1 12.3 %copy-start.4 = (f32[128,1024]{1,0:T(8,128)}, f32[128,1024]{1,0:T(8,128)S(1)}, u32[]{:S(2)}) copy-start(f32[128,1024]{1,0:T(8,128)S(1)} %fusion.16) | copy-start | bytes 1572868
  343.1 1.9 copy-start.2
  347.1 357.1 %all-reduce.3.cloned.1.call-start = ((), (), s32[]{:S(2)}) async-start(), calls=%async_computation.6 | async-start | bytes 8388608 | tf_op jit(solution)/shard_map/psum | solution.py:100
  357.2 406.2 %reduce-scatter.5.cloned.1.call-start = ((), (), s32[]{:S(2)}) async-start(), calls=%async_computation.5 | async-start | bytes 2359296 | tf_op jit(solution)/shard_map/reduce_scatter | solution.py:112
  557.9 1.3 copy-start.1
  704.2 3.3 copy-start.3
Sparse Core Ops, SparseCore 0:
  9.8 43.9 all-gather.2
  185.8 153.4 reduce-scatter.2
  347.2 85.2 all-gather.4
  438.5 265.6 all-reduce.2
  707.2 56.1 reduce-scatter.4
where the time goes:
time: 772 us; the launch traced here: 770 us
  waiting for transfers between devices  395 us (51%)
  other arithmetic  147 us (19%)
  matrix products  76.7 us (10%)
  blocking collectives  75.6 us (10%)
  local copies, waits for them, and re-layouts  61.2 us (8%)
  between operations  13.9 us (2%)
    reduce_scatter x1, waiting for transfers between devices, shards(): lax.psum_scatter(totals.reshape(col_count * TILE, F), 'col', scatter_dime...  154 us
    scatter-add x16, other arithmetic, advance(): return totals.at[placed].add(product)  126 us
    psum x1, blocking collectives, shards(): reduced = lax.psum((grad_in_w, grad_out_w, grad_gain), ('row', 'col'))  75.6 us
    all_gather x1, waiting for transfers between devices, shards(): lax.all_gather(grad_rows, 'col', axis=0, tiled=True)  75.2 us
    psum x1, waiting for transfers between devices, shards(): reduced = lax.psum((grad_in_w, grad_out_w, grad_gain), ('row', 'col'))  65 us
    reduce_scatter x1, waiting for transfers between devices, shards(): lax.psum_scatter(back.reshape(row_count * TILE, F), 'row', scatter_dimens...  54.3 us
    all_gather x1, waiting for transfers between devices, shards(): lax.all_gather(features, 'row', axis=0, tiled=True)  45.8 us
    dot_general x8, matrix products, advance(): jnp.einsum('sab,saf->sbf', weights_now, pieces, preferred_element_type=jn...  35.3 us
  transfers between devices with their start and end apart: 5, of which 5 were waited for; matrix products, arithmetic and copies ran while one was open for 19% of the time, Pallas kernels for 0%

commit v1 on v0

--- a/solution.py
+++ b/solution.py
@@ -98,7 +98,16 @@
     )
     grad_rows = grad_agg.astype(jnp.bfloat16)
     reduced = lax.psum((grad_in_w, grad_out_w, grad_gain), ("row", "col"))
-    grad_sources = lax.all_gather(grad_rows, "col", axis=0, tiled=True).reshape(col_count, TILE, F)
+    tell_positions_on = lambda local: jnp.concatenate(
+        lax.all_to_all(
+            jnp.stack([local] * lax.axis_size("col"), axis=0),
+            axis_name="col",
+            split_axis=0,
+            concat_axis=0,
+        ),
+        axis=0,
+    )
+    grad_sources = tell_positions_on(grad_rows).reshape(col_count, TILE, F)
     back = sweep(
         weights_all,
         row_ids_all,

time: 772 us -> 736 us (0.953)
  waiting for transfers between devices: 395 us -> 347 us
    all_to_all x0 -> x1, waiting for transfers between devices: none -> 94.6 us  [shards(): lax.all_to_all(jnp.stack([local] * lax.axis_size('col'), axis=0), axis_na...]
    all_gather x1 -> x0, waiting for transfers between devices: 75.2 us -> none  [shards(): lax.all_gather(grad_rows, 'col', axis=0, tiled=True)]
    psum x1, waiting for transfers between devices: 65 us -> 0.01 us  [shards(): reduced = lax.psum((grad_in_w, grad_out_w, grad_gain), ('row', 'col'))]
  transfers between devices with their start and end apart: 5 -> 5, of which waited for: 5 -> 4; matrix products, arithmetic and copies ran while one was open for 19% -> 20% of each run, Pallas kernels for 0% -> 0%
where the time goes in v1:
time: 736 us; the launch traced here: 734 us
  waiting for transfers between devices  347 us (47%)
  other arithmetic  146 us (20%)
  blocking collectives  78.6 us (11%)
  matrix products  76.7 us (10%)
  local copies, waits for them, and re-layouts  63.6 us (9%)
  between operations  13.9 us (2%)
    reduce_scatter x1, waiting for transfers between devices, shards(): lax.psum_scatter(totals.reshape(col_count * TILE, F), 'col', scatter_dime...  154 us
    scatter-add x16, other arithmetic, advance(): return totals.at[placed].add(product)  125 us
    all_to_all x1, waiting for transfers between devices, shards(): lax.all_to_all(jnp.stack([local] * lax.axis_size('col'), axis=0), axis_na...  94.6 us
    psum x1, blocking collectives, shards(): reduced = lax.psum((grad_in_w, grad_out_w, grad_gain), ('row', 'col'))  78.6 us
    reduce_scatter x1, waiting for transfers between devices, shards(): lax.psum_scatter(back.reshape(row_count * TILE, F), 'row', scatter_dimens...  52.2 us
    all_gather x1, waiting for transfers between devices, shards(): lax.all_gather(features, 'row', axis=0, tiled=True)  45.8 us
    dot_general x8, matrix products, advance(): jnp.einsum('sab,saf->sbf', weights_now, pieces, preferred_element_type=jn...  35.3 us
    gather x8, local copies, waits for them, and re-layouts, advance(): pieces = sources[row_ids]  33.6 us
  transfers between devices with their start and end apart: 5, of which 4 were waited for; matrix products, arithmetic and copies ran while one was open for 20% of the time, Pallas kernels for 0%

profile of v1, /device:TPU:32, one launch (start us, length us, event | category | flops | bytes accessed | tf_op | source)
XLA Modules:
  0.0 733.6 jit_solution(11256846463107069367)
XLA Ops:
  8.0 45.8 %all-gather.2.cloned.1.call-done = bf16[1024,512]{1,0:T(8,128)(2,1)} async-done(((bf16[128,512]{1,0:T(8,128)(2,1)}), bf16[1024,512]{1,0:T(8,128)(2,1)}) %all-gather.2.cloned.1.call-update) | async-done | bytes 1048592 | tf_op jit(solution)/shard_map/all_gather | solution.py:60
  53.8 4.3 broadcast_in_dim.90
  58.1 127.5 %while.26 = (s32[]{:T(128)}, f32[32,128,512]{2,1,0:T(8,128)}, s32[128]{0:T(128)S(1)}, s32[]{:T(128)}, bf16[128,128,128]{2,1,0:T(8,128)(2,1)}, /*index=5*/s32[128...) while((s32[]{:T(128)}, f32[32,128,512]{2,1,0:T(8,128)}, ...), condition=%wide.region_2.3_spmd, body=%wide.region_0.2_spmd.sunk | while | flops 270533856 | bytes 23597776 | solution.py:38
  60.8 3.7 convolution_select_fusion.4
  64.5 9.6 %scatter_fusion = f32[32,128,512]{2,1,0:T(8,128)} fusion(f32[32,128,512]{2,1,0:T(8,128)} %get-tuple-element.410, s32[16]{0:T(128)S(1)} %get-tuple-element.387, f32[16,128,512]{2,1,0:T(8,128)} %convolution_select_fusion.4), kind=kCustom, calls=%fused_computation.2.clone.1 | custom fusion | flops 1048576 | bytes 12582976 | tf_op jit(solution)/shard_map/while/body/eval_jaxpr/scatter-add | solution.py:36
  80.5 9.5 %scatter_fusion = f32[32,128,512]{2,1,0:T(8,128)} fusion(f32[32,128,512]{2,1,0:T(8,128)} %get-tuple-element.410, s32[16]{0:T(128)S(1)} %get-tuple-element.387, f32[16,128,512]{2,1,0:T(8,128)} %convolution_select_fusion.4), kind=kCustom, calls=%fused_computation.2.clone.1 | custom fusion | flops 1048576 | bytes 12582976 | tf_op jit(solution)/shard_map/while/body/eval_jaxpr/scatter-add | solution.py:36
  92.7 3.7 convolution_select_fusion.4
  96.4 9.4 %scatter_fusion = f32[32,128,512]{2,1,0:T(8,128)} fusion(f32[32,128,512]{2,1,0:T(8,128)} %get-tuple-element.410, s32[16]{0:T(128)S(1)} %get-tuple-element.387, f32[16,128,512]{2,1,0:T(8,128)} %convolution_select_fusion.4), kind=kCustom, calls=%fused_computation.2.clone.1 | custom fusion | flops 1048576 | bytes 12582976 | tf_op jit(solution)/shard_map/while/body/eval_jaxpr/scatter-add | solution.py:36
  112.3 9.5 %scatter_fusion = f32[32,128,512]{2,1,0:T(8,128)} fusion(f32[32,128,512]{2,1,0:T(8,128)} %get-tuple-element.410, s32[16]{0:T(128)S(1)} %get-tuple-element.387, f32[16,128,512]{2,1,0:T(8,128)} %convolution_select_fusion.4), kind=kCustom, calls=%fused_computation.2.clone.1 | custom fusion | flops 1048576 | bytes 12582976 | tf_op jit(solution)/shard_map/while/body/eval_jaxpr/scatter-add | solution.py:36
  124.5 3.7 convolution_select_fusion.4
  128.2 9.7 %scatter_fusion = f32[32,128,512]{2,1,0:T(8,128)} fusion(f32[32,128,512]{2,1,0:T(8,128)} %get-tuple-element.410, s32[16]{0:T(128)S(1)} %get-tuple-element.387, f32[16,128,512]{2,1,0:T(8,128)} %convolution_select_fusion.4), kind=kCustom, calls=%fused_computation.2.clone.1 | custom fusion | flops 1048576 | bytes 12582976 | tf_op jit(solution)/shard_map/while/body/eval_jaxpr/scatter-add | solution.py:36
  140.6 3.7 convolution_select_fusion.4
  144.3 9.5 %scatter_fusion = f32[32,128,512]{2,1,0:T(8,128)} fusion(f32[32,128,512]{2,1,0:T(8,128)} %get-tuple-element.410, s32[16]{0:T(128)S(1)} %get-tuple-element.387, f32[16,128,512]{2,1,0:T(8,128)} %convolution_select_fusion.4), kind=kCustom, calls=%fused_computation.2.clone.1 | custom fusion | flops 1048576 | bytes 12582976 | tf_op jit(solution)/shard_map/while/body/eval_jaxpr/scatter-add | solution.py:36
  156.5 3.7 convolution_select_fusion.4
  160.2 9.4 %scatter_fusion = f32[32,128,512]{2,1,0:T(8,128)} fusion(f32[32,128,512]{2,1,0:T(8,128)} %get-tuple-element.410, s32[16]{0:T(128)S(1)} %get-tuple-element.387, f32[16,128,512]{2,1,0:T(8,128)} %convolution_select_fusion.4), kind=kCustom, calls=%fused_computation.2.clone.1 | custom fusion | flops 1048576 | bytes 12582976 | tf_op jit(solution)/shard_map/while/body/eval_jaxpr/scatter-add | solution.py:36
  172.4 3.7 convolution_select_fusion.4
  176.0 9.5 %scatter_fusion = f32[32,128,512]{2,1,0:T(8,128)} fusion(f32[32,128,512]{2,1,0:T(8,128)} %get-tuple-element.410, s32[16]{0:T(128)S(1)} %get-tuple-element.387, f32[16,128,512]{2,1,0:T(8,128)} %convolution_select_fusion.4), kind=kCustom, calls=%fused_computation.2.clone.1 | custom fusion | flops 1048576 | bytes 12582976 | tf_op jit(solution)/shard_map/while/body/eval_jaxpr/scatter-add | solution.py:36
  185.6 153.8 %reduce-scatter.3.cloned.1.call-done = f32[128,512]{1,0:T(8,128)} async-done(((f32[4096,512]{1,0:T(8,128)}), f32[128,512]{1,0:T(8,128)}) %reduce-scatter.3.cloned.1.call-update) | async-done | bytes 262160 | tf_op jit(solution)/shard_map/reduce_scatter | solution.py:71
  349.0 7.0 all-to-all-start
  356.1 6.4 copy.15
  366.1 94.6 %all-to-all-done = bf16[32,128,512]{2,1,0:T(8,128)(2,1)} async-done(((bf16[32,128,512]{2,1,0:T(8,128)(2,1)}), bf16[32,128,512]{2,1,0:T(8,128)(2,1)}, u32[]{:S(2)}, u32[]{:S(2)}) %all-to-all-start) | async-done | bytes 4194336 | tf_op jit(solution)/shard_map/all_to_all | solution.py:102
  461.0 124.8 %while.27 = (s32[]{:T(128)}, f32[8,128,512]{2,1,0:T(8,128)S(1)}, s32[128]{0:T(128)S(1)}, s32[]{:T(128)}, bf16[128,128,128]{1,2,0:T(8,128)(2,1)}, /*index=5*/s32[...) while((s32[]{:T(128)}, f32[8,128,512]{2,1,0:T(8,128)S(1)}, ...), condition=%wide.region_10.11_spmd, body=%wide.region_8.10_spmd.sunk | while | flops 270533856 | bytes 23597776 | solution.py:38
  461.9 4.2 gather_fusion.1
  466.1 4.4 convolution_select_fusion.5
  470.5 6.1 scatter_fusion.1
  477.5 4.2 gather_fusion.1
  481.7 4.4 convolution_select_fusion.5
  486.1 6.1 scatter_fusion.1
  493.1 4.2 gather_fusion.1
  497.3 4.4 convolution_select_fusion.5
  501.7 6.1 scatter_fusion.1
  508.7 4.2 gather_fusion.1
  512.9 4.4 convolution_select_fusion.5
  517.3 6.1 scatter_fusion.1
  524.3 4.2 gather_fusion.1
  528.5 4.4 convolution_select_fusion.5
  532.9 6.1 scatter_fusion.1
  539.9 4.2 gather_fusion.1
  544.1 4.4 convolution_select_fusion.5
  548.5 6.2 scatter_fusion.1
  555.5 4.2 gather_fusion.1
  559.7 4.4 convolution_select_fusion.5
  564.1 6.1 scatter_fusion.1
  571.1 4.2 gather_fusion.1
  575.3 4.4 convolution_select_fusion.5
  579.7 6.2 scatter_fusion.1
  588.5 78.6 %psum.23 = f32[8,512]{1,0:T(8,128)S(1)} all-reduce(f32[8,512]{1,0:T(8,128)S(1)} %fusion.7), channel_id=1, replica_groups=mesh['row'=8,'col'=32] {'row','col'}, use_global_device_ids=true, to_apply=%region_14.15 | all-reduce | flops 4096 | bytes 32768 | tf_op jit(solution)/shard_map/psum | solution.py:100
  674.9 52.2 %reduce-scatter.5.cloned.1.call-done = f32[128,512]{1,0:T(8,128)} async-done(((f32[1024,512]{1,0:T(8,128)}), f32[128,512]{1,0:T(8,128)}) %reduce-scatter.5.cloned.1.call-update) | async-done | bytes 262160 | tf_op jit(solution)/shard_map/reduce_scatter | solution.py:121
  (106 shorter events, 60.2 us)
Async XLA Ops:
  7.2 335.7 %copy-start = (bf16[512,1024]{1,0:T(8,128)(2,1)S(1)}, bf16[512,1024]{1,0:T(8,128)(2,1)}, u32[]{:S(2)}) copy-start(bf16[512,1024]{1,0:T(8,128)(2,1)} %param.21) | copy-start | bytes 3145732
  7.2 46.6 %all-gather.2.cloned.1.call-start = ((), (), s32[]{:S(2)}) async-start(), calls=%async_computation.3 | async-start | bytes 1179648 | tf_op jit(solution)/shard_map/all_gather | solution.py:60
  7.9 331.4 %reduce-scatter.3.cloned.1.call-start = ((), (), s32[]{:S(2)}) async-start(), calls=%async_computation.4 | async-start | bytes 8650752 | tf_op jit(solution)/shard_map/reduce_scatter | solution.py:71
  53.8 4.3 copy-start.6
  53.8 4.3 copy-start.7
  185.5 156.1 %copy-start.8 = (f32[8,512]{1,0:T(8,128)S(1)}, f32[8,512]{1,0:T(8,128)}, u32[]{:S(2)}) copy-start(f32[8,512]{1,0:T(8,128)} %param.20) | copy-start | bytes 49156
  185.5 156.1 %copy-start.9 = (s32[128]{0:T(128)S(1)}, s32[128]{0:T(128)}, u32[]{:S(2)}) copy-start(s32[128]{0:T(128)} %param.19) | copy-start | bytes 1540
  185.6 157.6 %copy-start.5 = (bf16[128,512]{1,0:T(8,128)(2,1)S(1)}, bf16[128,512]{1,0:T(8,128)(2,1)}, u32[]{:S(2)}) copy-start(bf16[128,512]{1,0:T(8,128)(2,1)} %param.23) | copy-start | bytes 393220
  343.2 21.0 %copy-start.4 = (f32[128,1024]{1,0:T(8,128)}, f32[128,1024]{1,0:T(8,128)S(1)}, u32[]{:S(2)}) copy-start(f32[128,1024]{1,0:T(8,128)S(1)} %fusion.16) | copy-start | bytes 1572868
  343.2 1.9 copy-start.2
  349.0 111.8 %all-to-all-start = ((bf16[32,128,512]{2,1,0:T(8,128)(2,1)}), bf16[32,128,512]{2,1,0:T(8,128)(2,1)}, u32[]{:S(2)}, u32[]{:S(2)}) async-start(bf16[32,128,512]{2,1,0:T(8,128)(2,1)} %stack.2), calls=%async_computation.1 | async-start | bytes 8388608 | tf_op jit(solution)/shard_map/all_to_all | solution.py:102
  356.0 314.0 %all-reduce.3.cloned.1.call-start = ((), (), s32[]{:S(2)}) async-start(), calls=%async_computation.6 | async-start | bytes 8388608 | tf_op jit(solution)/shard_map/psum | solution.py:100
  366.1 361.0 %reduce-scatter.5.cloned.1.call-start = ((), (), s32[]{:S(2)}) async-start(), calls=%async_computation.5 | async-start | bytes 2359296 | tf_op jit(solution)/shard_map/reduce_scatter | solution.py:121
  585.9 1.3 copy-start.1
  670.1 3.3 copy-start.3
Sparse Core Ops, SparseCore 0:
  9.8 43.9 all-gather.1
  185.7 153.6 reduce-scatter.2
  366.2 301.7 all-reduce.2
  671.0 56.0 reduce-scatter.4
